TPU v7x, 32 devices: a whole 2x2x4 slice. The times are simulated.
32 devices in a mesh: ctx: 8 (over y, x, core), mp: 4 (over z).
Axes of the slice: x: 2, y: 2, z: 4, core: 2. Of those that a mesh axis runs over, the one named last changes fastest.
Arguments:
- queries: bfloat16 [128, 6144], P('ctx', 'mp'), may hold values from -9 to 9
- cache_keys: bfloat16 [8, 4096, 128], P('mp', 'ctx'), may hold values from -9 to 9, as said below
- cache_values: bfloat16 [8, 4096, 128], P('mp', 'ctx'), may hold values from -6 to 6, as said below
- new_keys: bfloat16 [8, 128, 128], P('mp', 'ctx'), may hold values from -6 to 6, as said below
- new_values: bfloat16 [8, 128, 128], P('mp', 'ctx'), may hold values from -6 to 6, as said below
- out_proj: bfloat16 [6144, 6144], P('mp', 'ctx'), may hold values from -3 to 3
- residual: bfloat16 [128, 6144], P('mp', 'ctx'), may hold values from -24 to 24
- norm_gain: bfloat16 [6144], replicated, may hold values from 0.5 to 1.5
- gate_proj: bfloat16 [8, 6144, 8192], P('ctx', None, 'mp'), may hold values from -0.078125 to 0.078125
- up_proj: bfloat16 [8, 6144, 8192], P('ctx', None, 'mp'), may hold values from -0.078125 to 0.078125
- down_proj: bfloat16 [8, 8192, 6144], P('ctx', 'mp'), may hold values from -0.09375 to 0.09375
- expert_ids: int32 [128, 2], replicated, may hold values from 0 to 7, all different within a row; in each aligned block of 128 rows (0 to 127, 128 to 255, ...) at most 64 rows name the same one
- route_logits: float32 [128, 2], replicated, may hold values from -6 to 6
Outputs:
- layer_out: bfloat16 [128, 6144], P('mp', 'ctx')
Inputs may be any that keep to these rules, and one draw needn't show every extreme that they name: `expert_ids`: each row names 2 different experts; at most 64 rows name one expert, a bound that some block reaches. `cache_keys`: slot s holds key head s * 1; slots of one key head are equal. `cache_values`: slot s holds value head s * 1; slots of one head are equal. `new_keys`: slot s holds key head s * 1; slots of one key head are equal. `new_values`: slot s holds value head s * 1; slots of one head are equal.
All inputs are finite; a program needn't handle non-finite values.
Results may differ from a plain program's by a relative error of at most 0.024.
Values may be sent and summed in bfloat16 or wider, within the bound.
No kernel may reach another device: no remote copies, remote signals or barrier semaphores. Data moves between devices by JAX's collectives and lax.ppermute only.
A program may use at most 128 MiB of HBM per device.

v0:
```python
import math
import jax
import jax.numpy as jnp
from jax import lax
from jax.sharding import PartitionSpec as P

D = 6144
EXPERTS = 8
TOP = 2
neg_big = -1e30
norm_eps = 1e-05


def route_slots(expert_ids):
    flat = expert_ids.reshape(-1)
    onehot = (flat[:, None] == jnp.arange(EXPERTS, dtype=jnp.int32)[None, :]).astype(jnp.int32)
    before = jnp.cumsum(onehot, axis=0, dtype=jnp.int32) - onehot
    return jnp.sum(before * onehot, axis=1, dtype=jnp.int32).reshape(expert_ids.shape)


def softmax_pieces(query_block, keys_local, values_local, allowed, scale):
    scores = (
        jnp.einsum("srd,skd->srk", query_block, keys_local, preferred_element_type=jnp.float32)
        * scale
    )
    scores = jnp.where(allowed[None, :, :], scores, neg_big)
    highest = jnp.max(scores, axis=2)
    expo = jnp.exp(scores - highest[:, :, None])
    denom = jnp.sum(expo, axis=2)
    summed = jnp.einsum(
        "srk,skd->srd", expo.astype(jnp.bfloat16), values_local, preferred_element_type=jnp.float32
    )
    return (highest, denom, summed)


def join_softmax(former, latter):
    highest = jnp.maximum(former[0], latter[0])
    right = jnp.exp(latter[0] - highest)
    denom = latter[1] * right
    summed = latter[2] * right[:, :, None]
    return (highest, denom, summed)


def on_device(
    queries,
    cache_keys,
    cache_values,
    new_keys,
    new_values,
    out_proj,
    residual,
    norm_gain,
    gate_proj,
    up_proj,
    down_proj,
    expert_ids,
    route_logits,
):
    ctx_count = lax.axis_size("ctx")
    mp_count = lax.axis_size("mp")
    ctx_index = lax.axis_index("ctx")
    mp_index = lax.axis_index("mp")
    tok_local = queries.shape[0]
    tokens = tok_local * ctx_count
    slot_local = cache_keys.shape[0]
    cache_local = cache_keys.shape[1]
    head_dim = cache_keys.shape[2]
    heads_local = queries.shape[1] // head_dim
    group_size = heads_local // slot_local
    width = cache_local + tok_local
    scale = 1.0 / math.sqrt(head_dim)
    d_local = out_proj.shape[1]
    key_value = jnp.stack(
        [
            jnp.concatenate([cache_keys, new_keys], axis=1),
            jnp.concatenate([cache_values, new_values], axis=1),
        ]
    )
    shaped = queries.reshape(tok_local, slot_local, group_size, head_dim)
    query_block = jnp.transpose(shaped, (1, 2, 0, 3)).reshape(
        slot_local, group_size * tok_local, head_dim
    )
    query_tok = ctx_index * tok_local + jnp.tile(jnp.arange(tok_local, dtype=jnp.int32), group_size)
    query_count = group_size * tok_local
    start_state = (
        jnp.full((slot_local, query_count), neg_big, jnp.float32),
        jnp.zeros((slot_local, query_count), jnp.float32),
        jnp.zeros((slot_local, query_count, head_dim), jnp.float32),
    )
    piece = lax.all_gather(key_value, "ctx", axis=2, tiled=True)
    position = jnp.arange(piece.shape[2], dtype=jnp.int32)
    shard = position // width
    within = position % width
    new_tok = shard * tok_local + within - cache_local
    allowed = (within[None, :] < cache_local) | (new_tok[None, :] <= query_tok[:, None])
    highest, denom, summed = join_softmax(
        start_state, softmax_pieces(query_block, piece[0], piece[1], allowed, scale)
    )
    shaped = (
        (summed / denom[:, :, None])
        .astype(jnp.bfloat16)
        .reshape(slot_local, group_size, tok_local, head_dim)
    )
    attn = jnp.transpose(shaped, (2, 0, 1, 3)).reshape(tok_local, heads_local * head_dim)
    projected = jnp.dot(
        lax.all_gather(attn, "ctx", axis=0, tiled=True),
        out_proj,
        preferred_element_type=jnp.float32,
    )
    res_rows = residual.shape[0]
    res_start = mp_index * res_rows
    current = lax.dynamic_slice_in_dim(projected, res_start, res_rows, 0)
    projected = lax.dynamic_update_slice_in_dim(
        projected, current + residual.astype(jnp.float32), res_start, 0
    )
    hidden = lax.psum(projected.astype(jnp.bfloat16), "mp")
    capacity = tokens * TOP // 4
    slots = route_slots(expert_ids)
    per_row = max(1, EXPERTS // mp_count)
    first_expert = mp_index * EXPERTS // mp_count
    own_expert = (mp_index * ctx_count + ctx_index) * EXPERTS // (ctx_count * mp_count)
    local = own_expert - first_expert
    row_experts = first_expert + jnp.arange(per_row, dtype=jnp.int32)
    match = expert_ids[None, :, :] == row_experts[:, None, None]
    place = jnp.where(match, slots[None, :, :], capacity)
    table = place[:, :, :, None] == jnp.arange(capacity, dtype=jnp.int32)[None, None, None, :]
    pick = jnp.any(table, axis=2)
    packed = jnp.einsum(
        "rtc,td->rcd", pick.astype(jnp.bfloat16), hidden, preferred_element_type=jnp.float32
    ).astype(jnp.bfloat16)
    gate_local = gate_proj[0]
    up_local = up_proj[0]
    down_local = down_proj[0]
    chosen = lax.dynamic_index_in_dim(
        lax.all_gather(packed, "ctx", axis=2, tiled=True), local, 0, keepdims=False
    )
    wide = chosen.astype(jnp.float32)
    gains = norm_gain.astype(jnp.float32)
    scaled = (wide * gains[None, :]).astype(jnp.bfloat16)
    gate_sum = jnp.dot(scaled, gate_local, preferred_element_type=jnp.float32)
    up_sum = jnp.dot(scaled, up_local, preferred_element_type=jnp.float32)
    gate_sum, up_sum, squares = (gate_sum, up_sum, jnp.sum(wide * wide, axis=1))
    rms = lax.rsqrt(squares / D + norm_eps)
    act = (jax.nn.silu(rms[:, None] * gate_sum) * (rms[:, None] * up_sum)).astype(jnp.bfloat16)
    part = lax.dot_general(
        down_local, act, (((0,), (1,)), ((), ())), preferred_element_type=jnp.float32
    )
    returned = lax.psum_scatter(
        jnp.concatenate(
            [jnp.where(local == which, part, 0.0) for which in range(per_row)], axis=1
        ).astype(jnp.bfloat16),
        "ctx",
        scatter_dimension=0,
        tiled=True,
    ).astype(jnp.float32)
    weights = jax.nn.softmax(route_logits, axis=1)
    combine = jnp.sum(jnp.where(table, weights[None, :, :, None], 0.0), axis=2)
    moe = jnp.einsum(
        "drc,rtc->td",
        returned.reshape(d_local, per_row, capacity),
        combine,
        precision=lax.Precision.HIGHEST,
        preferred_element_type=jnp.float32,
    )
    share = lax.psum_scatter(
        moe.astype(jnp.bfloat16), "mp", scatter_dimension=0, tiled=True
    ).astype(jnp.float32)
    own_hidden = lax.dynamic_slice_in_dim(hidden, res_start, res_rows, 0).astype(jnp.float32)
    return (own_hidden + share).astype(jnp.bfloat16)


def solution(mesh):
    placed = (
        P("ctx", "mp"),
        P("mp", "ctx", None),
        P("mp", "ctx", None),
        P("mp", "ctx", None),
        P("mp", "ctx", None),
        P("mp", "ctx"),
        P("mp", "ctx"),
        P(),
        P("ctx", None, "mp"),
        P("ctx", None, "mp"),
        P("ctx", "mp", None),
        P(),
        P(),
    )
    return jax.shard_map(
        on_device, mesh=mesh, in_specs=placed, out_specs=P("mp", "ctx"), check_vma=False
    )
```

profile of v0, /device:TPU:0, one launch (start us, length us, event | category | flops | bytes accessed | tf_op | source)
XLA Modules:
  0.0 234.1 jit_solution(1601538211125830650)
XLA Ops:
  6.5 0.0 copy-start
  6.5 0.0 all-gather.3.cloned.1.call-start
  6.5 1.3 maximum_bitcast_fusion
  7.8 0.9 pad_maximum_fusion.1
  8.7 0.0 all-gather.3.cloned.1.call-update
  8.7 0.0 all-reduce.2.cloned.1.call-start
  8.8 0.8 copy.30
  9.5 0.1 eq.70
  9.7 0.1 eq.66
  9.8 0.6 reduce-window.6
  10.4 0.2 slice_reduce_fusion
  10.7 0.1 fusion.64
  10.8 0.1 broadcast_in_dim.67
  10.9 0.1 copy.32
  11.0 0.1 add.99
  11.1 0.1 reshape.149
  11.3 0.3 compare_or_fusion
  11.6 37.6 %all-gather.3.cloned.1.call-done = bf16[2,2,4224,128]{3,2,1,0:T(8,128)(2,1)} async-done(((bf16[2,2,528,128]{3,2,1,0:T(8,128)(2,1)}), bf16[2,2,4224,128]{3,2,1,0:T(8,128)(2,1)}) %all-gather.3.cloned.1.call-update) | async-done | bytes 4325392 | tf_op jit(solution)/shard_map/all_gather | solution.py:90
  49.3 2.8 %fusion.74 = (f32[2,96]{1,0:T(2,128)S(1)}, f32[2,96,4224]{2,1,0:T(8,128)S(1)}) fusion(bf16[2,96,128]{2,1,0:T(8,128)(2,1)S(1)} %bitcast.87, bf16[2,2,4224,128]{3,2,1,0:T(8,128)(2,1)} %all-gather.3.cloned.1.call-done, pred[96,4224]{1,0:T(8,128)(4,1)S(1)} %compare_or_fusion), kind=kOutput, calls=%fused_computation.88 | convolution fusion | flops 210050880 | bytes 5862144 | tf_op jit(solution)/shard_map/srd,skd->srk/dot_general | solution.py:23
  52.1 0.6 fusion.8
  52.7 0.8 fusion.36
  53.5 0.0 copy-start.3
  53.5 0.0 copy-start.6
  53.5 0.0 copy-start.4
  53.6 0.1 reshape.152
  53.7 9.6 %all_gather.10 = bf16[128,1536]{1,0:T(8,128)(2,1)S(1)} all-gather(bf16[16,1536]{1,0:T(8,128)(2,1)S(1)} %reshape.152), channel_id=1, replica_groups=mesh['ctx'=8,'mp'=4] {'ctx'}, dimensions={0}, use_global_device_ids=true | all-gather | bytes 442368 | tf_op jit(solution)/shard_map/all_gather | solution.py:106
  63.2 0.5 fusion.81
  63.7 0.7 convert_element_type.59
  64.4 0.0 all-reduce.2.cloned.1.call-update
  64.4 0.0 all-gather.5.cloned.1.call-start
  64.5 0.0 copy-done.6
  64.5 0.1 compare_select_fusion
  64.6 34.8 %all-reduce.2.cloned.1.call-done = bf16[128,768]{1,0:T(8,128)(2,1)} async-done(((bf16[128,768]{1,0:T(8,128)(2,1)}), bf16[128,768]{1,0:T(8,128)(2,1)}) %all-reduce.2.cloned.1.call-update) | async-done | bytes 196624 | tf_op jit(solution)/shard_map/psum | solution.py:116
  99.5 1.8 convolution_convert_fusion
  101.2 0.0 all-gather.5.cloned.1.call-update
  101.3 0.2 reduce-scatter.3.cloned.1.call-start
  101.6 25.4 %all-gather.5.cloned.1.call-done = bf16[2,64,6144]{2,1,0:T(8,128)(2,1)} async-done(((bf16[2,64,768]{2,1,0:T(8,128)(2,1)}), bf16[2,64,6144]{2,1,0:T(8,128)(2,1)}) %all-gather.5.cloned.1.call-update) | async-done | bytes 1572880 | tf_op jit(solution)/shard_map/all_gather | solution.py:135
  127.0 1.4 fusion.27
  128.4 13.7 %fusion.10 = f32[64,2048]{1,0:T(8,128)} fusion(bf16[1,6144,2048]{2,1,0:T(8,128)(2,1)} %param.21, f32[6144]{0:T(1024)S(1)} %convert_element_type.65, bf16[2,64,6144]{2,1,0:T(8,128)(2,1)} %all-gather.5.cloned.1.call-done, s32[]{:T(128)S(6)} %select_n.86, f32[64]{0:T(128)S(1)} %add_rsqrt_fusion), kind=kOutput, calls=%fused_computation.12 | convolution fusion | flops 1611923456 | bytes 26501380 | tf_op jit(solution)/shard_map/dot_general | solution.py:140
  142.1 21.4 %fusion.39 = (bf16[6144,64]{0,1:T(8,128)(2,1)S(1)}, bf16[6144,64]{0,1:T(8,128)(2,1)}) fusion(pred[]{:T(512)S(6)} %eq.77, pred[]{:T(512)S(6)} %eq.78, bf16[1,2048,6144]{2,1,0:T(8,128)(2,1)} %param.23, bf16[1,6144,2048]{2,1,0:T(8,128)(2,1)} %param.22, f32[6144]{0:T(1024)S(1)} %convert_element_type.65, bf16[2,64,6144]{2,1,0:T(8,128)(2,1)} %all-gather.5.cloned.1.call-done, ...), kind=kOutput, calls=%fused_computation.34 | convolution fusion | flops 3224109056 | bytes 53240072 | tf_op jit(solution)/shard_map/dot_general | solution.py:145
  163.5 2.4 %pad_maximum_fusion = bf16[6144,128]{0,1:T(8,128)(2,1)} fusion(bf16[6144,64]{0,1:T(8,128)(2,1)} %get-tuple-element.6, bf16[6144,64]{0,1:T(8,128)(2,1)S(1)} %get-tuple-element.5), kind=kLoop, calls=%fused_computation.25 | loop fusion | flops 3145728 | bytes 3145728 | tf_op jit(solution)/shard_map/concatenate | solution.py:149
  165.9 0.0 reduce-scatter.3.cloned.1.call-update
  166.0 0.0 reduce-scatter.5.cloned.1.call-start
  166.1 38.5 %reduce-scatter.3.cloned.1.call-done = bf16[768,128]{0,1:T(8,128)(2,1)} async-done(((bf16[6144,128]{0,1:T(8,128)(2,1)}), bf16[768,128]{0,1:T(8,128)(2,1)}) %reduce-scatter.3.cloned.1.call-update) | async-done | bytes 196624 | tf_op jit(solution)/shard_map/reduce_scatter | solution.py:148
  204.6 2.0 fusion.29
  206.5 0.0 reduce-scatter.5.cloned.1.call-update
  206.6 19.6 %reduce-scatter.5.cloned.1.call-done = bf16[32,768]{1,0:T(8,128)(2,1)} async-done(((bf16[128,768]{1,0:T(8,128)(2,1)}), bf16[32,768]{1,0:T(8,128)(2,1)}) %reduce-scatter.5.cloned.1.call-update) | async-done | bytes 49168 | tf_op jit(solution)/shard_map/reduce_scatter | solution.py:165
  226.1 1.5 add_convert_fusion
  (32 shorter events, 0.3 us)
Async XLA Ops:
  6.5 56.7 %copy-start = (bf16[1536,768]{1,0:T(8,128)(2,1)S(1)}, bf16[1536,768]{1,0:T(8,128)(2,1)}, u32[]{:S(2)}) copy-start(bf16[1536,768]{1,0:T(8,128)(2,1)} %param.18) | copy-start | bytes 7077892
  6.5 4.6 %copy-start.2 = (bf16[16,1536]{1,0:T(8,128)(2,1)S(1)}, bf16[16,1536]{1,0:T(8,128)(2,1)}, u32[]{:S(2)}) copy-start(bf16[16,1536]{1,0:T(8,128)(2,1)} %param.13) | copy-start | bytes 147460
  6.5 42.7 %all-gather.3.cloned.1.call-start = ((), (), s32[]{:S(2)}) async-start(), calls=%async_computation.2 | async-start | bytes 4866048 | tf_op jit(solution)/shard_map/all_gather | solution.py:90
  8.7 90.8 %all-reduce.2.cloned.1.call-start = ((), (), s32[]{:S(2)}) async-start(), calls=%async_computation.3 | async-start | bytes 393216 | tf_op jit(solution)/shard_map/psum | solution.py:116
  49.3 3.4 %slice-start = ((s8[4325376]{0:T(1024)(128)(4,1)}), s8[4194304]{0:T(1024)(128)(4,1)S(1)}, s32[]{:S(2)}) async-start(s8[4325376]{0:T(1024)(128)(4,1)} %bitcast.89), calls=%async_computation.7 | async-start | bytes 8388608
  49.3 3.4 %slice-start.1 = ((s8[4325376]{0:T(1024)(128)(4,1)}), s8[131072]{0:T(1024)(128)(4,1)S(1)}, s32[]{:S(2)}) async-start(s8[4325376]{0:T(1024)(128)(4,1)} %bitcast.89), calls=%async_computation.8 | async-start | bytes 262144
  53.5 10.2 %copy-start.3 = (bf16[32,768]{1,0:T(8,128)(2,1)S(1)}, bf16[32,768]{1,0:T(8,128)(2,1)}, u32[]{:S(2)}) copy-start(bf16[32,768]{1,0:T(8,128)(2,1)} %param.19) | copy-start | bytes 147460
  53.5 11.0 %copy-start.6 = (s32[128,2]{0,1:T(2,128)S(1)}, s32[128,2]{0,1:T(2,128)}, u32[]{:S(2)}) copy-start(s32[128,2]{0,1:T(2,128)} %param.24) | copy-start | bytes 3076
  53.5 48.0 %copy-start.4 = (bf16[6144]{0:T(1024)(128)(2,1)S(1)}, bf16[6144]{0:T(1024)(128)(2,1)}, u32[]{:S(2)}) copy-start(bf16[6144]{0:T(1024)(128)(2,1)} %param.20) | copy-start | bytes 36868
  64.4 62.5 %all-gather.5.cloned.1.call-start = ((), (), s32[]{:S(2)}) async-start(), calls=%async_computation.4 | async-start | bytes 1769472 | tf_op jit(solution)/shard_map/all_gather | solution.py:135
  101.3 103.3 %reduce-scatter.3.cloned.1.call-start = ((), (), s32[]{:S(2)}) async-start(), calls=%async_computation.5 | async-start | bytes 1769472 | tf_op jit(solution)/shard_map/reduce_scatter | solution.py:148
  142.1 85.5 %copy-start.1 = (bf16[1536,768]{1,0:T(8,128)(2,1)S(1)}, bf16[1536,768]{1,0:T(8,128)(2,1)}, u32[]{:S(2)}) copy-start(bf16[1536,768]{1,0:T(8,128)(2,1)} %param.18) | copy-start | bytes 7077892
  163.5 2.5 %copy-start.5 = (f32[128,2]{0,1:T(2,128)S(1)}, f32[128,2]{0,1:T(2,128)}, u32[]{:S(2)}) copy-start(f32[128,2]{0,1:T(2,128)} %param.25) | copy-start | bytes 3076
  166.0 60.2 %reduce-scatter.5.cloned.1.call-start = ((), (), s32[]{:S(2)}) async-start(), calls=%async_computation.6 | async-start | bytes 245760 | tf_op jit(solution)/shard_map/reduce_scatter | solution.py:165
Sparse Core Ops, SparseCore 0:
  9.3 39.9 all-gather.2
  64.6 34.8 all-reduce.1
  101.5 25.3 all-gather.4
  166.1 38.4 reduce-scatter.2
  206.8 19.3 reduce-scatter.4
where the time goes:
time: 235 us; the launch traced here: 234 us
  waiting for transfers between devices  156 us (66%)
  matrix products  42.9 us (18%)
  between operations  13.4 us (6%)
  other arithmetic  10 us (4%)
  blocking collectives  9.55 us (4%)
    reduce_scatter x1, waiting for transfers between devices, on_device(): lax.psum_scatter(jnp.concatenate([jnp.where(local == which, part, 0.0) fo...  38.5 us
    all_gather x1, waiting for transfers between devices, on_device(): piece = lax.all_gather(key_value, 'ctx', axis=2, tiled=True)  37.6 us
    psum x1, waiting for transfers between devices, on_device(): hidden = lax.psum(projected.astype(jnp.bfloat16), 'mp')  34.8 us
    all_gather x1, waiting for transfers between devices, on_device(): lax.all_gather(packed, 'ctx', axis=2, tiled=True)  25.4 us
    dot_general x1, matrix products, on_device(): lax.dot_general(down_local, act, (((0,), (1,)), ((), ())), preferred_elem...  21.4 us
    reduce_scatter x1, waiting for transfers between devices, on_device(): lax.psum_scatter(moe.astype(jnp.bfloat16), 'mp', scatter_dimension=0, til...  19.6 us
    dot_general x1, matrix products, on_device(): gate_sum = jnp.dot(scaled, gate_local, preferred_element_type=jnp.float32)  13.7 us
    all_gather x1, blocking collectives, on_device(): lax.all_gather(attn, 'ctx', axis=0, tiled=True)  9.55 us
  transfers between devices with their start and end apart: 5, of which 5 were waited for; matrix products, arithmetic and copies ran while one was open for 1% of the time, Pallas kernels for 0%

commit v1 on v0

--- a/solution.py
+++ b/solution.py
@@ -9,6 +9,12 @@
 TOP = 2
 neg_big = -1e30
 norm_eps = 1e-05
+
+
+def summed_here(block, axis):
+    parts = lax.all_gather(block, axis, axis=0, tiled=False)
+    total = parts.sum(axis=0)
+    return total
 
 
 def route_slots(expert_ids):
@@ -113,7 +119,7 @@
     projected = lax.dynamic_update_slice_in_dim(
         projected, current + residual.astype(jnp.float32), res_start, 0
     )
-    hidden = lax.psum(projected.astype(jnp.bfloat16), "mp")
+    hidden = summed_here(projected.astype(jnp.bfloat16), "mp")
     capacity = tokens * TOP // 4
     slots = route_slots(expert_ids)
     per_row = max(1, EXPERTS // mp_count)

time: 235 us -> 216 us (0.919)
  waiting for transfers between devices: 156 us -> 120 us
  blocking collectives: 9.55 us -> 29.1 us
    psum x1 -> x0, waiting for transfers between devices: 34.8 us -> none  [on_device(): hidden = lax.psum(projected.astype(jnp.bfloat16), 'mp')]
    all_gather x0 -> x1, blocking collectives: none -> 19.5 us  [summed_here(): parts = lax.all_gather(block, axis, axis=0, tiled=False)]
  transfers between devices with their start and end apart: 5 -> 4, of which waited for: 5 -> 4; matrix products, arithmetic and copies ran while one was open for 1% -> 1% of each run, Pallas kernels for 0% -> 0%
where the time goes in v1:
time: 216 us
  waiting for transfers between devices  120 us (56%)
  matrix products  42 us (19%)
  blocking collectives  29.1 us (13%)
  between operations  13.4 us (6%)
  other arithmetic  9.46 us (4%)
    reduce_scatter x1, waiting for transfers between devices, on_device(): lax.psum_scatter(jnp.concatenate([jnp.where(local == which, part, 0.0) fo...  38.5 us
    all_gather x1, waiting for transfers between devices, on_device(): piece = lax.all_gather(key_value, 'ctx', axis=2, tiled=True)  37.5 us
    all_gather x1, waiting for transfers between devices, on_device(): lax.all_gather(packed, 'ctx', axis=2, tiled=True)  24.1 us
    dot_general x1, matrix products, on_device(): lax.dot_general(down_local, act, (((0,), (1,)), ((), ())), preferred_elem...  21.4 us
    all_gather x1, blocking collectives, summed_here(): parts = lax.all_gather(block, axis, axis=0, tiled=False)  19.5 us
    reduce_scatter x1, waiting for transfers between devices, on_device(): lax.psum_scatter(moe.astype(jnp.bfloat16), 'mp', scatter_dimension=0, til...  19.5 us
    dot_general x1, matrix products, on_device(): gate_sum = jnp.dot(scaled, gate_local, preferred_element_type=jnp.float32)  13.7 us
    all_gather x1, blocking collectives, on_device(): lax.all_gather(attn, 'ctx', axis=0, tiled=True)  9.54 us
  transfers between devices with their start and end apart: 4, of which 4 were waited for; matrix products, arithmetic and copies ran while one was open for 1% of the time, Pallas kernels for 0%

profile of v1, /device:TPU:0, one launch (start us, length us, event | category | flops | bytes accessed | tf_op | source)
XLA Modules:
  0.0 215.6 jit_solution(14895729790930824606)
XLA Ops:
  6.5 0.0 copy-start
  6.5 1.3 maximum_bitcast_fusion
  7.8 0.9 pad_maximum_fusion.1
  8.7 0.0 all-gather.4.cloned.1.call-update
  8.7 0.0 all-gather.6.cloned.1.call-start
  8.8 0.8 copy.30
  9.6 0.1 eq.70
  9.7 0.1 eq.66
  9.9 0.6 reduce-window.6
  10.5 0.2 slice_reduce_fusion
  10.7 0.1 fusion.64
  10.8 0.1 broadcast_in_dim.67
  11.0 0.1 copy.32
  11.0 0.1 add.97
  11.1 0.1 reshape.149
  11.3 0.0 copy-done.6
  11.3 0.1 compare_select_fusion
  11.4 0.3 compare_or_fusion
  11.8 37.5 %all-gather.4.cloned.1.call-done = bf16[2,2,4224,128]{3,2,1,0:T(8,128)(2,1)} async-done(((bf16[2,2,528,128]{3,2,1,0:T(8,128)(2,1)}), bf16[2,2,4224,128]{3,2,1,0:T(8,128)(2,1)}) %all-gather.4.cloned.1.call-update) | async-done | bytes 4325392 | tf_op jit(solution)/shard_map/all_gather | solution.py:96
  49.3 2.8 %fusion.74 = (f32[2,96]{1,0:T(2,128)S(1)}, f32[2,96,4224]{2,1,0:T(8,128)S(1)}) fusion(bf16[2,96,128]{2,1,0:T(8,128)(2,1)S(1)} %bitcast.89, bf16[2,2,4224,128]{3,2,1,0:T(8,128)(2,1)} %all-gather.4.cloned.1.call-done, pred[96,4224]{1,0:T(8,128)(4,1)S(1)} %compare_or_fusion), kind=kOutput, calls=%fused_computation.88 | convolution fusion | flops 210050880 | bytes 5862144 | tf_op jit(solution)/shard_map/srd,skd->srk/dot_general | solution.py:29
  52.1 0.6 fusion.8
  52.7 0.0 slice-done
  52.7 0.0 slice-done.1
  52.7 0.7 fusion.36
  53.4 0.0 copy-start.3
  53.5 0.1 reshape.152
  53.6 9.5 %all_gather.16 = bf16[128,1536]{1,0:T(8,128)(2,1)S(1)} all-gather(bf16[16,1536]{1,0:T(8,128)(2,1)S(1)} %reshape.152), channel_id=1, replica_groups=mesh['ctx'=8,'mp'=4] {'ctx'}, dimensions={0}, use_global_device_ids=true | all-gather | bytes 442368 | tf_op jit(solution)/shard_map/all_gather | solution.py:112
  63.1 0.0 copy-done
  63.1 0.5 fusion.81
  63.7 19.5 %all-gather = bf16[512,768]{1,0:T(8,128)(2,1)S(1)} all-gather(bf16[128,768]{1,0:T(8,128)(2,1)S(1)} %convert_element_type.61), channel_id=2, replica_groups=mesh['ctx'=8,'mp'=4] {'mp'}, dimensions={0}, use_global_device_ids=true | all-gather | bytes 983040 | tf_op jit(solution)/shard_map/all_gather | solution.py:15
  83.2 0.1 reduce_sum.58
  83.3 0.9 convolution_convert_fusion
  84.2 0.0 all-gather.6.cloned.1.call-update
  84.2 0.2 reduce-scatter.3.cloned.1.call-start
  84.5 24.1 %all-gather.6.cloned.1.call-done = bf16[2,64,6144]{2,1,0:T(8,128)(2,1)} async-done(((bf16[2,64,768]{2,1,0:T(8,128)(2,1)}), bf16[2,64,6144]{2,1,0:T(8,128)(2,1)}) %all-gather.6.cloned.1.call-update) | async-done | bytes 1572880 | tf_op jit(solution)/shard_map/all_gather | solution.py:141
  108.5 1.4 fusion.27
  110.0 13.7 %fusion.10 = f32[64,2048]{1,0:T(8,128)} fusion(bf16[1,6144,2048]{2,1,0:T(8,128)(2,1)} %param.21, f32[6144]{0:T(1024)S(1)} %convert_element_type.67, bf16[2,64,6144]{2,1,0:T(8,128)(2,1)} %all-gather.6.cloned.1.call-done, s32[]{:T(128)S(6)} %select_n.86, f32[64]{0:T(128)S(1)} %add_rsqrt_fusion), kind=kOutput, calls=%fused_computation.12 | convolution fusion | flops 1611923456 | bytes 26501380 | tf_op jit(solution)/shard_map/dot_general | solution.py:146
  123.7 21.4 %fusion.39 = (bf16[6144,64]{0,1:T(8,128)(2,1)S(1)}, bf16[6144,64]{0,1:T(8,128)(2,1)}) fusion(pred[]{:T(512)S(6)} %eq.77, pred[]{:T(512)S(6)} %eq.78, bf16[1,2048,6144]{2,1,0:T(8,128)(2,1)} %param.23, bf16[1,6144,2048]{2,1,0:T(8,128)(2,1)} %param.22, f32[6144]{0:T(1024)S(1)} %convert_element_type.67, bf16[2,64,6144]{2,1,0:T(8,128)(2,1)} %all-gather.6.cloned.1.call-done, ...), kind=kOutput, calls=%fused_computation.34 | convolution fusion | flops 3224109056 | bytes 53240072 | tf_op jit(solution)/shard_map/dot_general | solution.py:151
  145.1 2.4 %pad_maximum_fusion = bf16[6144,128]{0,1:T(8,128)(2,1)} fusion(bf16[6144,64]{0,1:T(8,128)(2,1)} %get-tuple-element.6, bf16[6144,64]{0,1:T(8,128)(2,1)S(1)} %get-tuple-element.5), kind=kLoop, calls=%fused_computation.25 | loop fusion | flops 3145728 | bytes 3145728 | tf_op jit(solution)/shard_map/concatenate | solution.py:155
  147.5 0.0 reduce-scatter.3.cloned.1.call-update
  147.5 0.0 reduce-scatter.5.cloned.1.call-start
  147.6 0.0 copy-done.5
  147.7 38.5 %reduce-scatter.3.cloned.1.call-done = bf16[768,128]{0,1:T(8,128)(2,1)} async-done(((bf16[6144,128]{0,1:T(8,128)(2,1)}), bf16[768,128]{0,1:T(8,128)(2,1)}) %reduce-scatter.3.cloned.1.call-update) | async-done | bytes 196624 | tf_op jit(solution)/shard_map/reduce_scatter | solution.py:154
  186.2 2.0 fusion.29
  188.1 0.0 reduce-scatter.5.cloned.1.call-update
  188.2 19.5 %reduce-scatter.5.cloned.1.call-done = bf16[32,768]{1,0:T(8,128)(2,1)} async-done(((bf16[128,768]{1,0:T(8,128)(2,1)}), bf16[32,768]{1,0:T(8,128)(2,1)}) %reduce-scatter.5.cloned.1.call-update) | async-done | bytes 49168 | tf_op jit(solution)/shard_map/reduce_scatter | solution.py:171
  207.6 1.4 add_convert_fusion
  209.1 0.0 copy-done.1
  (31 shorter events, 0.3 us)
Async XLA Ops:
  6.5 56.6 %copy-start = (bf16[1536,768]{1,0:T(8,128)(2,1)S(1)}, bf16[1536,768]{1,0:T(8,128)(2,1)}, u32[]{:S(2)}) copy-start(bf16[1536,768]{1,0:T(8,128)(2,1)} %param.18) | copy-start | bytes 7077892
  6.5 4.8 %copy-start.6 = (s32[128,2]{0,1:T(2,128)S(1)}, s32[128,2]{0,1:T(2,128)}, u32[]{:S(2)}) copy-start(s32[128,2]{0,1:T(2,128)} %param.24) | copy-start | bytes 3076
  6.5 4.6 %copy-start.2 = (bf16[16,1536]{1,0:T(8,128)(2,1)S(1)}, bf16[16,1536]{1,0:T(8,128)(2,1)}, u32[]{:S(2)}) copy-start(bf16[16,1536]{1,0:T(8,128)(2,1)} %param.13) | copy-start | bytes 147460
  6.5 42.7 %all-gather.4.cloned.1.call-start = ((), (), s32[]{:S(2)}) async-start(), calls=%async_computation.2 | async-start | bytes 4866048 | tf_op jit(solution)/shard_map/all_gather | solution.py:96
  8.7 99.8 %all-gather.6.cloned.1.call-start = ((), (), s32[]{:S(2)}) async-start(), calls=%async_computation.3 | async-start | bytes 1769472 | tf_op jit(solution)/shard_map/all_gather | solution.py:141
  49.3 3.4 %slice-start = ((s8[4325376]{0:T(1024)(128)(4,1)}), s8[4194304]{0:T(1024)(128)(4,1)S(1)}, s32[]{:S(2)}) async-start(s8[4325376]{0:T(1024)(128)(4,1)} %bitcast.91), calls=%async_computation.6 | async-start | bytes 8388608
  49.3 3.4 %slice-start.1 = ((s8[4325376]{0:T(1024)(128)(4,1)}), s8[131072]{0:T(1024)(128)(4,1)S(1)}, s32[]{:S(2)}) async-start(s8[4325376]{0:T(1024)(128)(4,1)} %bitcast.91), calls=%async_computation.7 | async-start | bytes 262144
  53.4 10.2 %copy-start.3 = (bf16[32,768]{1,0:T(8,128)(2,1)S(1)}, bf16[32,768]{1,0:T(8,128)(2,1)}, u32[]{:S(2)}) copy-start(bf16[32,768]{1,0:T(8,128)(2,1)} %param.19) | copy-start | bytes 147460
  63.1 21.4 %copy-start.4 = (bf16[6144]{0:T(1024)(128)(2,1)S(1)}, bf16[6144]{0:T(1024)(128)(2,1)}, u32[]{:S(2)}) copy-start(bf16[6144]{0:T(1024)(128)(2,1)} %param.20) | copy-start | bytes 36868
  84.2 102.0 %reduce-scatter.3.cloned.1.call-start = ((), (), s32[]{:S(2)}) async-start(), calls=%async_computation.4 | async-start | bytes 1769472 | tf_op jit(solution)/shard_map/reduce_scatter | solution.py:154
  123.7 85.4 %copy-start.1 = (bf16[1536,768]{1,0:T(8,128)(2,1)S(1)}, bf16[1536,768]{1,0:T(8,128)(2,1)}, u32[]{:S(2)}) copy-start(bf16[1536,768]{1,0:T(8,128)(2,1)} %param.18) | copy-start | bytes 7077892
  145.1 2.5 %copy-start.5 = (f32[128,2]{0,1:T(2,128)S(1)}, f32[128,2]{0,1:T(2,128)}, u32[]{:S(2)}) copy-start(f32[128,2]{0,1:T(2,128)} %param.25) | copy-start | bytes 3076
  147.5 60.1 %reduce-scatter.5.cloned.1.call-start = ((), (), s32[]{:S(2)}) async-start(), calls=%async_computation.5 | async-start | bytes 245760 | tf_op jit(solution)/shard_map/reduce_scatter | solution.py:171
Sparse Core Ops, SparseCore 0:
  9.3 39.9 all-gather.3
  84.3 24.1 all-gather.5
  147.7 38.4 reduce-scatter.2
  188.3 19.3 reduce-scatter.4
